TPU v7x, 512 devices: a whole 4x4x16 slice. The times are simulated.
512 devices in a mesh: tm: 32 (over y, z_lo), lon: 16 (over x, z_hi, core).
Axes of the slice: x: 4, y: 4, z: 16 (z_hi: 2, z_lo: 8; z = z_hi * 8 + z_lo), core: 2. Of those that a mesh axis runs over, the one named last changes fastest.
Arguments:
- field: bfloat16 [4096, 288, 512], P('tm', 'lon'), may hold values from -15 to 15
- omega: bfloat16 [288, 512, 64], P('lon'), may hold values from -0.015625 to 0.015625
Outputs:
- projected: bfloat16 [4096, 288, 512], P('tm', 'lon')
- series: float32 [4096, 64], P('tm')
All inputs are finite; a program needn't handle non-finite values.
Results may differ from a plain program's by a relative error of at most 0.0082.
Values may be sent and summed in bfloat16 or wider, within the bound.
A program may use at most 64 MiB of HBM per device.

v0:
```python
import math

import jax
import jax.numpy as jnp
from jax import lax
from jax.sharding import PartitionSpec as P

NLAT = 32
NVAR = 16
HALF = 15
RANK = 64


def with_halo(block, sides, width, periodic):
    for axis, dim in sides:
        count = lax.axis_size(axis)
        forward = [(i, i + 1) for i in range(count - 1)]
        if periodic:
            forward.append((count - 1, 0))
        backward = [(target, source) for source, target in forward]
        low = lax.ppermute(
            lax.slice_in_dim(block, block.shape[dim] - width, None, axis=dim), axis, forward
        )
        high = lax.ppermute(lax.slice_in_dim(block, 0, width, axis=dim), axis, backward)
        block = jnp.concatenate([low, block, high], axis=dim)
    return block


def band_taps(half):
    offsets = jnp.arange(-half, half + 1).astype(jnp.float32)
    safe = jnp.where(offsets == 0, 1.0, offsets)
    core = (jnp.sin(2.0 * math.pi * safe / 3.0) - jnp.sin(2.0 * math.pi * safe / 30.0)) / (
        math.pi * safe
    )
    core = jnp.where(offsets == 0, 2.0 * (1.0 / 3.0 - 1.0 / 30.0), core)
    spread = math.pi * safe / (half + 1)
    sigma = jnp.where(offsets == 0, 1.0, jnp.sin(spread) / spread)
    return (core * sigma).astype(jnp.bfloat16)


def local(field, omega):
    days, lon_dev, cols = field.shape
    width = lon_dev * cols
    extended = with_halo(field, (("tm", 0),), HALF, False)
    extended = with_halo(extended, (("lon", 1),), 1, True)
    taps = band_taps(HALF).astype(jnp.float32)
    row_index = lax.broadcasted_iota(jnp.int32, (days, days + 2 * HALF), 0)
    col_index = lax.broadcasted_iota(jnp.int32, (days, days + 2 * HALF), 1)
    offset = col_index - row_index
    tap_index = jnp.arange(2 * HALF + 1, dtype=jnp.int32)
    toeplitz = jnp.sum(jnp.where(offset[:, :, None] == tap_index, taps, 0.0), axis=-1).astype(
        jnp.bfloat16
    )
    filtered = jnp.einsum("ij,jlc->ilc", toeplitz, extended, preferred_element_type=jnp.float32)
    across = filtered[:, :-2] + 2.0 * filtered[:, 1:-1] + filtered[:, 2:]
    grid = across.reshape(days, lon_dev, NVAR, NLAT)
    lat_pad = jnp.pad(grid, ((0, 0), (0, 0), (0, 0), (1, 1)))
    smooth = (lat_pad[..., :-2] + 2.0 * lat_pad[..., 1:-1] + lat_pad[..., 2:]) * 0.0625
    anomalies = smooth.reshape(days, width).astype(jnp.bfloat16)
    flat_omega = omega.reshape(width, RANK)
    partial_sketch = jnp.dot(anomalies, flat_omega, preferred_element_type=jnp.float32)
    sketch = lax.psum(partial_sketch, "lon")
    local_gram = jnp.dot(sketch.T, sketch, precision=lax.Precision.HIGHEST)
    gram = lax.psum(local_gram, "tm")
    lower = jnp.linalg.cholesky(gram)
    basis = jax.scipy.linalg.solve_triangular(lower, sketch.T, lower=True).T
    series = basis * math.sqrt(days * lax.axis_size("tm"))
    basis_b = basis.astype(jnp.bfloat16)
    terms = jnp.einsum("ts,tk->sk", anomalies, basis_b, preferred_element_type=jnp.float32)
    patterns = lax.psum(terms, "tm").astype(jnp.bfloat16)
    projected = jnp.einsum(
        "tk,sk->ts", basis_b, patterns, preferred_element_type=jnp.float32
    ).astype(jnp.bfloat16)
    return (projected.reshape(days, lon_dev, cols), series)


def solution(mesh):
    in_specs = (P("tm", "lon", None), P("lon", None, None))
    out_specs = (P("tm", "lon", None), P("tm", None))
    return jax.shard_map(local, mesh=mesh, in_specs=in_specs, out_specs=out_specs, check_vma=False)
```

profile of v0, /device:TPU:4, one launch (start us, length us, event | category | flops | bytes accessed | tf_op | source)
XLA Modules:
  0.0 712.1 jit_solution(13577348520286733900)
XLA Ops:
  0.6 1.3 fusion.27
  1.9 3.8 collective-permute-start
  5.8 1.3 collective-permute-start.1
  7.1 1.4 copy.20
  8.6 3.5 collective-permute-done
  12.0 10.3 %collective-permute-done.1 = bf16[15,18,512]{2,0,1:T(8,128)(2,1)S(1)} collective-permute-done((bf16[15,18,512]{2,0,1:T(8,128)(2,1)S(1)}, bf16[15,18,512]{2,0,1:T(8,128)(2,1)S(1)}, u32[]{:S(2)}, u32[]{:S(2)}) %collective-permute-start.1) | collective-permute-done | bytes 276512 | tf_op jit(solution)/shard_map/ppermute | solution.py:24
  22.4 1.9 collective-permute-start.2
  24.3 13.3 %collective-permute-start.3 = (bf16[158,1,512]{2,0,1:T(8,128)(2,1)S(1)}, bf16[158,1,512]{2,0,1:T(8,128)(2,1)S(1)}, u32[]{:S(2)}, u32[]{:S(2)}) collective-permute-start(bf16[158,1,512]{2,0,1:T(8,128)(2,1)S(1)} %get-tuple-element.9), channel_id=1, source_target_pairs={{1,0},{2,1},{3,2},{4,3},{5,4},{6,5},{7,6},{8,7},{9,8},{10,9},{11,1... | collective-permute-start | bytes 485384 | tf_op jit(solution)/shard_map/ppermute | solution.py:24
  37.9 0.9 collective-permute-done.2
  38.8 6.9 collective-permute-done.3
  45.7 1.0 fusion.5
  46.6 2.8 slice_add_fusion
  49.5 6.1 copy.13
  55.6 6.7 fusion.3
  62.3 1.2 fusion.29
  63.5 125.3 %psum.21 = f32[128,64]{0,1:T(8,128)S(1)} all-reduce(f32[128,64]{0,1:T(8,128)} %fusion.29), channel_id=1, replica_groups=mesh['tm'=32,'lon'=16] {'lon'}, use_global_device_ids=true, to_apply=%region_1.2 | all-reduce | flops 8192 | bytes 65536 | tf_op jit(solution)/shard_map/psum | solution.py:62
  188.9 231.2 %psum.22 = f32[64,64]{0,1:T(8,128)S(1)} all-reduce(f32[64,64]{0,1:T(8,128)S(1)} %fusion.28), channel_id=1, replica_groups=mesh['tm'=32,'lon'=16] {'tm'}, use_global_device_ids=true, to_apply=%region_2.3 | all-reduce | flops 4096 | bytes 32768 | tf_op jit(solution)/shard_map/psum | solution.py:64
  420.3 5.8 cholesky.16
  427.4 4.9 custom-call.7
  432.3 0.9 broadcast_multiply_fusion
  433.2 2.3 fusion.23
  435.6 269.1 %all-reduce.2 = bf16[9216,64]{0,1:T(8,128)(2,1)S(1)} all-reduce(f32[9216,64]{0,1:T(8,128)} %fusion.23), channel_id=1, replica_groups=mesh['tm'=32,'lon'=16] {'tm'}, use_global_device_ids=true, to_apply=%region_5.6 | all-reduce | flops 589824 | bytes 3538944 | tf_op jit(solution)/shard_map/psum | solution.py:70
  705.4 2.4 copy.17
  707.9 4.3 copy.18
  (13 shorter events, 2.9 us)
Async XLA Ops:
  0.6 21.6 %copy-start = (bf16[128,18,512]{2,0,1:T(8,128)(2,1)S(1)}, bf16[128,18,512]{2,0,1:T(8,128)(2,1)}, u32[]{:S(2)}) copy-start(bf16[128,18,512]{2,0,1:T(8,128)(2,1)} %param.2) | copy-start | bytes 7077892
  1.9 10.1 %collective-permute-start = (bf16[15,18,512]{2,0,1:T(8,128)(2,1)S(1)}, bf16[15,18,512]{2,0,1:T(8,128)(2,1)S(1)}, u32[]{:S(2)}, u32[]{:S(2)}) collective-permute-start(bf16[15,18,512]{2,0,1:T(8,128)(2,1)S(1)} %get-tuple-element.10), channel_id=1, source_target_pairs={{0,16},{16,32},{32,48},{48,64},{64,80},{80,96},{96,112},{112,128},... | collective-permute-start | bytes 829448 | tf_op jit(solution)/shard_map/ppermute | solution.py:21
  5.8 16.5 %collective-permute-start.1 = (bf16[15,18,512]{2,0,1:T(8,128)(2,1)S(1)}, bf16[15,18,512]{2,0,1:T(8,128)(2,1)S(1)}, u32[]{:S(2)}, u32[]{:S(2)}) collective-permute-start(bf16[15,18,512]{2,0,1:T(8,128)(2,1)S(1)} %get-tuple-element.11), channel_id=1, source_target_pairs={{16,0},{32,16},{48,32},{64,48},{80,64},{96,80},{112,96},{128,112},... | collective-permute-start | bytes 829448 | tf_op jit(solution)/shard_map/ppermute | solution.py:24
  22.4 16.4 %collective-permute-start.2 = (bf16[158,1,512]{2,0,1:T(8,128)(2,1)S(1)}, bf16[158,1,512]{2,0,1:T(8,128)(2,1)S(1)}, u32[]{:S(2)}, u32[]{:S(2)}) collective-permute-start(bf16[158,1,512]{2,0,1:T(8,128)(2,1)S(1)} %get-tuple-element.8), channel_id=1, source_target_pairs={{0,1},{1,2},{2,3},{3,4},{4,5},{5,6},{6,7},{7,8},{8,9},{9,10},{10,1... | collective-permute-start | bytes 485384 | tf_op jit(solution)/shard_map/ppermute | solution.py:21
  24.3 21.4 %collective-permute-start.3 = (bf16[158,1,512]{2,0,1:T(8,128)(2,1)S(1)}, bf16[158,1,512]{2,0,1:T(8,128)(2,1)S(1)}, u32[]{:S(2)}, u32[]{:S(2)}) collective-permute-start(bf16[158,1,512]{2,0,1:T(8,128)(2,1)S(1)} %get-tuple-element.9), channel_id=1, source_target_pairs={{1,0},{2,1},{3,2},{4,3},{5,4},{6,5},{7,6},{8,7},{9,8},{10,9},{11,1... | collective-permute-start | bytes 485384 | tf_op jit(solution)/shard_map/ppermute | solution.py:24
where the time goes:
time: 713 us; the launch traced here: 712 us
  blocking collectives  626 us (88%)
  other arithmetic  22.1 us (3%)
  waiting for transfers between devices  21.5 us (3%)
  starting transfers between devices  20.3 us (3%)
  local copies, waits for them, and re-layouts  15.6 us (2%)
    psum x1, blocking collectives, local(): patterns = lax.psum(terms, 'tm').astype(jnp.bfloat16)  269 us
    psum x1, blocking collectives, local(): gram = lax.psum(local_gram, 'tm')  231 us
    psum x1, blocking collectives, local(): sketch = lax.psum(partial_sketch, 'lon')  125 us
    ppermute x2, waiting for transfers between devices, with_halo(): lax.ppermute(lax.slice_in_dim(block, 0, width, axis=dim), axis, backward)  17.2 us
    ppermute x2, starting transfers between devices, with_halo(): lax.ppermute(lax.slice_in_dim(block, 0, width, axis=dim), axis, backward)  14.5 us
  transfers between devices with their start and end apart: 4, of which 4 were waited for; matrix products, arithmetic and copies ran while one was open for 0% of the time, Pallas kernels for 0%

commit v1 on v0

v1 whole, which is shorter than its diff:
```python
import math

import jax
import jax.numpy as jnp
import ml_dtypes
import numpy as np
from jax import lax
from jax.experimental import pallas as pl
from jax.experimental.pallas import tpu as pltpu
from jax.sharding import PartitionSpec as P

NLAT = 32
HALF = 15
RANK = 64
NY, NZ, NX = 4, 8, 4
HI = lax.Precision.HIGHEST
MESH = pl.DeviceIdType.MESH


def toeplitz_blocks():
    offsets = np.arange(-HALF, HALF + 1).astype(np.float64)
    safe = np.where(offsets == 0, 1.0, offsets)
    core = (np.sin(2.0 * math.pi * safe / 3.0) - np.sin(2.0 * math.pi * safe / 30.0)) / (math.pi * safe)
    core = np.where(offsets == 0, 2.0 * (1.0 / 3.0 - 1.0 / 30.0), core)
    spread = math.pi * safe / (HALF + 1)
    sigma = np.where(offsets == 0, 1.0, np.sin(spread) / spread)
    taps = (core * sigma).astype(np.float32).astype(ml_dtypes.bfloat16).astype(np.float32)
    rows = np.arange(384)[:, None] - 128
    cols = np.arange(128)[None, :]
    diff = rows - cols
    inside = np.abs(diff) <= HALF
    return np.where(inside, taps[np.clip(diff + HALF, 0, 2 * HALF)], 0.0).astype(np.float32)


def halves(value):
    high = value.astype(jnp.bfloat16)
    low = (value - high.astype(jnp.float32)).astype(jnp.bfloat16)
    return jnp.concatenate([high, low], axis=0)


def contract_last(a, b, precision=None):
    return lax.dot_general(a, b, (((1,), (1,)), ((), ())), precision=precision, preferred_element_type=jnp.float32)


def contract_first(a, b, precision=None):
    return lax.dot_general(a, b, (((0,), (0,)), ((), ())), precision=precision, preferred_element_type=jnp.float32)


def matmul(a, b, precision=None):
    return jnp.dot(a, b, precision=precision, preferred_element_type=jnp.float32)


def lat_smooth(tile):
    lane = lax.broadcasted_iota(jnp.int32, tile.shape, tile.ndim - 1) % NLAT
    left = jnp.where(lane == 0, 0.0, pltpu.roll(tile, 1, tile.ndim - 1))
    right = jnp.where(lane == NLAT - 1, 0.0, pltpu.roll(tile, 127, tile.ndim - 1))
    return left + 2.0 * tile + right


def kernel(
    field, omega, toeplitz, patterns_out, basis_out, series_out,
    fhalo, osm, va, cbuf, xbuf, zq, edges, edge_in, gbuf, gin, ysend, yrecv, zsend, zrecv, gathered, elim,
    halo_s, halo_r, core_s, core_r, x_s, x_r, zq_s, zq_r, edge_s, edge_r, g_s, g_r, y_s, y_r, z_s, z_r,
    az_s, az_r, ay_s, ay_r,
):
    bands = field.shape[0]
    tm = lax.axis_index("tm")
    lon = lax.axis_index("lon")
    days_blocks = NY * NZ
    y, z = tm // NZ, tm % NZ
    nlon = 16
    next_lon, prev_lon = (lon + 1) % nlon, (lon + nlon - 1) % nlon
    core_lon = lon + 1 - 2 * (lon % 2)
    zh_lon = lon + 2 - 4 * ((lon // 2) % 2)
    x = lon // 4
    x_lons = [((x + d) % NX) * 4 + lon % 4 for d in range(1, NX)]
    next_tm, prev_tm = (tm + 1) % days_blocks, (tm + days_blocks - 1) % days_blocks
    y_tms = [((y + d) % NY) * NZ + z for d in range(1, NY)]
    z_tms = [y * NZ + (z + d) % NZ for d in range(1, NZ)]

    def remote(src, dst, send, recv, to_tm, to_lon):
        copy = pltpu.make_async_remote_copy(
            src_ref=src, dst_ref=dst, send_sem=send, recv_sem=recv,
            device_id=(to_tm, to_lon), device_id_type=MESH,
        )
        copy.start()
        return copy

    barrier = pltpu.get_barrier_semaphore()
    partners = [(tm, next_lon), (tm, prev_lon), (tm, zh_lon)]
    partners += [(tm, other) for other in x_lons]
    partners += [(t, l) for t in (next_tm, prev_tm) for l in (lon, zh_lon)]
    partners += [(t, lon) for t in y_tms + z_tms]
    for partner in partners:
        pl.semaphore_signal(barrier, inc=1, device_id=partner, device_id_type=MESH)

    osm[0] = jnp.zeros_like(osm[0])
    osm[bands + 1] = jnp.zeros_like(osm[0])

    def smooth_omega(l, carry):
        for c in range(4):
            tile = omega[l, :, c * 128:(c + 1) * 128].astype(jnp.float32)
            osm[l + 1, :, c * 128:(c + 1) * 128] = lat_smooth(tile) * 0.0625
        return carry

    lax.fori_loop(0, bands, smooth_omega, 0)
    pl.semaphore_wait(barrier, len(partners))

    up = remote(field.at[bands - 1], fhalo.at[0], halo_s.at[0], halo_r.at[0], tm, next_lon)
    down = remote(field.at[0], fhalo.at[1], halo_s.at[1], halo_r.at[1], tm, prev_lon)

    def sketch_term(l, acc):
        weights = osm[l] + 2.0 * osm[l + 1] + osm[l + 2]
        return acc + contract_last(halves(weights), field[l])

    acc = lax.fori_loop(0, bands, sketch_term, jnp.zeros((2 * RANK, 128), jnp.float32))
    up.wait()
    acc = acc + contract_last(halves(osm[1]), fhalo[0])
    down.wait()
    acc = acc + contract_last(halves(osm[bands]), fhalo[1])

    cbuf[0] = acc[:RANK] + acc[RANK:]
    copy = remote(cbuf.at[0], cbuf.at[1], core_s, core_r, tm, core_lon)
    copy.wait()
    xbuf[x] = cbuf[0] + cbuf[1]
    copies = [
        remote(xbuf.at[x], xbuf.at[x], x_s.at[i], x_r.at[i], tm, other) for i, other in enumerate(x_lons)
    ]
    for copy in copies:
        copy.wait()
    total = (xbuf[0] + xbuf[1]) + (xbuf[2] + xbuf[3])
    zq[0] = total
    full = remote(zq.at[0], zq.at[1], zq_s, zq_r, tm, zh_lon)
    lane16 = lax.broadcasted_iota(jnp.int32, (16, 128), 1)
    first = jnp.zeros((16, 128), jnp.float32)
    last = jnp.zeros((16, 128), jnp.float32)
    for g in range(4):
        piece = total[16 * g:16 * (g + 1)]
        mine = lane16 // 32 == g
        first = jnp.where(mine, piece if g == 0 else pltpu.roll(piece, 32 * g, 1), first)
        last = jnp.where(mine, piece if g == 3 else pltpu.roll(piece, 32 * (g + 1), 1), last)
    edges[0] = last
    edges[1] = first
    copies = []
    for side, to_tm in ((0, next_tm), (1, prev_tm)):
        for part, to_lon in ((0, lon), (1, zh_lon)):
            i = 2 * side + part
            copies.append(remote(edges.at[side], edge_in.at[i], edge_s.at[i], edge_r.at[i], to_tm, to_lon))
    full.wait()
    for copy in copies:
        copy.wait()
    before = edge_in[0] + edge_in[1]
    after = edge_in[2] + edge_in[3]
    low, high = [], []
    for g in range(4):
        low.append(jnp.where(lane16 >= 96, before if g == 3 else pltpu.roll(before, 96 - 32 * g, 1), 0.0))
        high.append(jnp.where(lane16 < 32, after if g == 0 else pltpu.roll(after, 128 - 32 * g, 1), 0.0))
    has_low = (tm > 0).astype(jnp.float32)
    has_high = (tm < days_blocks - 1).astype(jnp.float32)
    low = jnp.concatenate(low, axis=0) * has_low
    high = jnp.concatenate(high, axis=0) * has_high
    raw = zq[0] + zq[1]

    t_low, t_mid, t_high = (toeplitz[128 * i:128 * (i + 1)] for i in range(3))
    sketch = matmul(low, t_low, HI) + matmul(raw, t_mid, HI) + matmul(high, t_high, HI)
    sketch_low = (matmul(low, t_mid, HI) + matmul(raw, t_high, HI)) * has_low
    sketch_high = (matmul(raw, t_low, HI) + matmul(high, t_mid, HI)) * has_high
    back = matmul(sketch_low, t_low, HI) + matmul(sketch, t_mid, HI) + matmul(sketch_high, t_high, HI)
    gram = contract_last(sketch, sketch, HI)
    gbuf[0] = jnp.concatenate([gram, jnp.zeros((RANK, 64), jnp.float32)], axis=1)

    back2 = halves(back)

    def term(block):
        both = matmul(back2, block)
        return both[:RANK] + both[RANK:]

    va[0] = term(fhalo[0])
    va[bands + 1] = term(fhalo[1])

    def pattern_term(l, carry):
        va[l + 1] = term(field[l])
        return carry

    lax.fori_loop(0, bands, pattern_term, 0)

    def pack(pair, carry):
        l = 2 * pair
        one, two, three, four = va[l], va[l + 1], va[l + 2], va[l + 3]
        even = one + 2.0 * two + three
        odd = two + 2.0 * three + four
        for c in range(NY):
            for k in range(NZ):
                rows, cols = slice(8 * k, 8 * k + 8), slice(128 * c, 128 * c + 128)
                ysend[c, k, pair] = jnp.concatenate([even[rows, cols], odd[rows, cols]], axis=0).astype(jnp.bfloat16)
        return carry

    lax.fori_loop(0, bands // 2, pack, 0)

    y_copies = []
    for d in range(1, NY):
        y_copies.append(
            remote(ysend.at[(y + d) % NY], yrecv.at[d - 1], y_s.at[d - 1], y_r.at[d - 1], y_tms[d - 1], lon)
        )

    steps = [(1, z, 1), (2, z, 2), (4, z, 4), (1, y, NZ), (2, y, 2 * NZ)]
    for i, (bit, coord, stride) in enumerate(steps):
        to_tm = tm + stride - 2 * stride * ((coord // bit) % 2)
        copy = remote(gbuf.at[i], gin.at[i], g_s.at[i], g_r.at[i], to_tm, lon)
        copy.wait()
        gbuf[i + 1] = gbuf[i] + gin[i]

    for copy in y_copies:
        copy.wait()

    def sum_y(k, carry):
        value = ysend[y, k].astype(jnp.float32)
        for d in range(NY - 1):
            value = value + yrecv[d, k].astype(jnp.float32)
        zsend[k] = value.astype(jnp.bfloat16)
        return carry

    lax.fori_loop(0, NZ, sum_y, 0)
    z_copies = []
    for d in range(1, NZ):
        z_copies.append(
            remote(zsend.at[(z + d) % NZ], zrecv.at[d - 1], z_s.at[d - 1], z_r.at[d - 1], z_tms[d - 1], lon)
        )

    lane = lax.broadcasted_iota(jnp.int32, (RANK, 128), 1)
    row_of = lax.broadcasted_iota(jnp.int32, (RANK, 128), 0)
    elim[...] = jnp.where(lane == row_of + RANK, 1.0, gbuf[len(steps)])

    def eliminate(j, carry):
        matrix = elim[...]
        row = elim[pl.ds(j, 1), :]
        column = jnp.sum(jnp.where(lane == j, matrix, 0.0), axis=1, keepdims=True)
        pivot = jnp.sum(jnp.where(lane[:1] == j, row, 0.0), axis=1, keepdims=True)
        factor = jnp.where(row_of[:, :1] > j, column / pivot, 0.0)
        elim[...] = matrix - factor * row
        return carry

    lax.fori_loop(0, RANK, eliminate, 0)
    matrix = elim[...]
    diagonal = jnp.sum(jnp.where(lane == row_of, matrix, 0.0), axis=1, keepdims=True)
    inverse = (matrix / jnp.sqrt(diagonal))[:, RANK:]
    basis = matmul(inverse, sketch, HI)
    series_out[...] = basis * math.sqrt(128 * days_blocks)
    basis_out[...] = contract_first(inverse, basis, HI).astype(jnp.bfloat16)

    for copy in z_copies:
        copy.wait()
    value = zsend[z].astype(jnp.float32)
    for d in range(NZ - 1):
        value = value + zrecv[d].astype(jnp.float32)
    value = lat_smooth(value.reshape(bands // 2 * 16, 128)) * 0.0625
    gathered[y, z] = value.reshape(bands // 2, 16, 128).astype(jnp.bfloat16)

    az = [
        remote(gathered.at[y, z], gathered.at[y, z], az_s.at[i], az_r.at[i], other, lon)
        for i, other in enumerate(z_tms)
    ]
    ay = []

    def over_y(i, k):
        for d in range(1, NY):
            ay.append(
                remote(gathered.at[y, k], gathered.at[y, k], ay_s.at[i, d - 1], ay_r.at[i, d - 1], y_tms[d - 1], lon)
            )

    over_y(0, z)
    for d in (1, 7, 2, 6, 3, 5, 4):
        az[d - 1].wait_recv()
        over_y(d, (z + NZ - d) % NZ)
    for copy in az:
        copy.wait_send()
    for copy in ay:
        copy.wait()

    def unpack(pair, carry):
        for c in range(NY):
            both = [gathered[c, k, pair].astype(jnp.float32) for k in range(NZ)]
            cols = slice(128 * c, 128 * c + 128)
            for i in range(2):
                rows = jnp.concatenate([block[8 * i:8 * i + 8] for block in both], axis=0)
                patterns_out[2 * pair + i, :, cols] = rows.astype(jnp.bfloat16)
        return carry

    lax.fori_loop(0, bands // 2, unpack, 0)


def project(basis, patterns, out):
    for i in range(patterns.shape[0]):
        out[i] = contract_first(basis[...], patterns[i]).astype(jnp.bfloat16)


def local(field, omega):
    days, bands, cols = field.shape
    pairs = bands // 2
    f32, bf16 = jnp.float32, jnp.bfloat16
    dma = pltpu.SemaphoreType.DMA
    chunk = (pairs, 16, 128)
    vmem = pl.BlockSpec(memory_space=pltpu.VMEM)
    patterns, basis, series = pl.pallas_call(
        kernel,
        out_shape=(
            jax.ShapeDtypeStruct((bands, RANK, cols), bf16),
            jax.ShapeDtypeStruct((RANK, days), bf16),
            jax.ShapeDtypeStruct((RANK, days), f32),
        ),
        in_specs=[vmem] * 3,
        out_specs=(vmem,) * 3,
        scratch_shapes=[
            pltpu.VMEM((2, days, cols), bf16),
            pltpu.VMEM((bands + 2, RANK, cols), f32),
            pltpu.VMEM((bands + 2, RANK, cols), f32),
            pltpu.VMEM((2, RANK, days), f32),
            pltpu.VMEM((NX, RANK, days), f32),
            pltpu.VMEM((2, RANK, days), f32),
            pltpu.VMEM((2, 16, days), f32),
            pltpu.VMEM((4, 16, days), f32),
            pltpu.VMEM((6, RANK, 128), f32),
            pltpu.VMEM((5, RANK, 128), f32),
            pltpu.VMEM((NY, NZ) + chunk, bf16),
            pltpu.VMEM((NY - 1, NZ) + chunk, bf16),
            pltpu.VMEM((NZ,) + chunk, bf16),
            pltpu.VMEM((NZ - 1,) + chunk, bf16),
            pltpu.VMEM((NY, NZ) + chunk, bf16),
            pltpu.VMEM((RANK, 128), f32),
            dma((2,)), dma((2,)), dma, dma, dma((3,)), dma((3,)), dma, dma, dma((4,)), dma((4,)),
            dma((5,)), dma((5,)), dma((3,)), dma((3,)), dma((7,)), dma((7,)), dma((7,)), dma((7,)),
            dma((8, 3)), dma((8, 3)),
        ],
        compiler_params=pltpu.CompilerParams(collective_id=0, has_side_effects=True),
        name="subspace",
    )(jnp.transpose(field, (1, 0, 2)), jnp.transpose(omega, (0, 2, 1)), jnp.asarray(toeplitz_blocks()))
    step = 3
    projected = pl.pallas_call(
        project,
        grid=(bands // step,),
        out_shape=jax.ShapeDtypeStruct((bands, days, cols), bf16),
        in_specs=[
            pl.BlockSpec((RANK, days), lambda i: (0, 0)),
            pl.BlockSpec((step, RANK, cols), lambda i: (i, 0, 0)),
        ],
        out_specs=pl.BlockSpec((step, days, cols), lambda i: (i, 0, 0)),
        name="project",
    )(basis, patterns)
    return jnp.transpose(projected, (1, 0, 2)), series.T


def solution(mesh):
    in_specs = (P("tm", "lon", None), P("lon", None, None))
    out_specs = (P("tm", "lon", None), P("tm", None))
    return jax.shard_map(local, mesh=mesh, in_specs=in_specs, out_specs=out_specs, check_vma=False)
```

time: 713 us -> 117 us (0.16)
  the two profiles are of different devices: /device:TPU:4 before, /device:TPU:2 now
where the time goes in v1:
time: 117 us
  Pallas kernels  116 us (99%)
    pallas_call x1, Pallas kernels, local(): pl.pallas_call(kernel, out_shape=(jax.ShapeDtypeStruct((bands, RANK, cols...  110 us
    pallas_call x1, Pallas kernels, local(): pl.pallas_call(project, grid=(bands // step,), out_shape=jax.ShapeDtypeSt...  5.34 us

profile of v1, /device:TPU:2, one launch (start us, length us, event | category | flops | bytes accessed | tf_op | source)
XLA Modules:
  0.0 116.8 jit_solution(3285782629036323241)
XLA Ops:
  0.6 110.2 %subspace.1 = (bf16[18,64,512]{2,1,0:T(8,128)(2,1)}, bf16[64,128]{1,0:T(8,128)(2,1)}, f32[64,128]{1,0:T(8,128)}) custom-call(bf16[18,128,512]{2,1,0:T(8,128)(2,1)} %bitcast.4, bf16[18,64,512]{2,1,0:T(8,128)(2,1)} %bitcast.6, f32[384,128]{1,0:T(8,128)} %constant.2.clone.toeplitz), custom_call_target="tpu_custom_call" | custom-call | tf_op jit(solution)/shard_map/subspace/pallas_call | solution.py:304
  110.9 0.0 copy-start
  110.9 5.3 %project.1 = bf16[18,128,512]{2,1,0:T(8,128)(2,1)} custom-call(bf16[64,128]{1,0:T(8,128)(2,1)} %get-tuple-element.5.basis, bf16[18,64,512]{2,1,0:T(8,128)(2,1)} %get-tuple-element.6.patterns), custom_call_target="tpu_custom_call" | custom-call | tf_op jit(solution)/shard_map/project/pallas_call | solution.py:338
  116.2 0.0 copy-done
  116.2 0.6 copy.6
Async XLA Ops:
  110.9 5.4 %copy-start = (f32[64,128]{1,0:T(8,128)S(1)}, f32[64,128]{1,0:T(8,128)}, u32[]{:S(2)}) copy-start(f32[64,128]{1,0:T(8,128)} %get-tuple-element.7) | copy-start | bytes 98308

commit v2 on v1

--- a/solution.py
+++ b/solution.py
@@ -59,9 +59,9 @@
 
 def kernel(
     field, omega, toeplitz, patterns_out, basis_out, series_out,
-    fhalo, osm, va, cbuf, xbuf, zq, edges, edge_in, gbuf, gin, ysend, yrecv, zsend, zrecv, gathered, elim,
-    halo_s, halo_r, core_s, core_r, x_s, x_r, zq_s, zq_r, edge_s, edge_r, g_s, g_r, y_s, y_r, z_s, z_r,
-    az_s, az_r, ay_s, ay_r,
+    ohalo, osm, fy, ubuf, cbuf, xbuf, zq, edges, edge_in, gbuf, gin, zsend, zrecv, lon_edge, lon_in, gathered, rims, elim,
+    halo_s, halo_r, core_s, core_r, x_s, x_r, zq_s, zq_r, edge_s, edge_r, g_s, g_r, f_s, f_r, u_s, u_r, z_s, z_r,
+    le_s, le_r, az_s, az_r, ay_s, ay_r, rz_s, rz_r, ry_s, ry_r,
 ):
     bands = field.shape[0]
     tm = lax.axis_index("tm")
@@ -104,20 +104,31 @@
         return carry
 
     lax.fori_loop(0, bands, smooth_omega, 0)
-    pl.semaphore_wait(barrier, len(partners))
-
-    up = remote(field.at[bands - 1], fhalo.at[0], halo_s.at[0], halo_r.at[0], tm, next_lon)
-    down = remote(field.at[0], fhalo.at[1], halo_s.at[1], halo_r.at[1], tm, prev_lon)
 
     def sketch_term(l, acc):
         weights = osm[l] + 2.0 * osm[l + 1] + osm[l + 2]
         return acc + contract_last(halves(weights), field[l])
 
     acc = lax.fori_loop(0, bands, sketch_term, jnp.zeros((2 * RANK, 128), jnp.float32))
+    pl.semaphore_wait(barrier, len(partners))
+
+    up = remote(omega.at[bands - 1], ohalo.at[0], halo_s.at[0], halo_r.at[0], tm, next_lon)
+    down = remote(omega.at[0], ohalo.at[1], halo_s.at[1], halo_r.at[1], tm, prev_lon)
+    f_copies = []
+    for d in range(1, NY):
+        cols = pl.ds(pl.multiple_of(128 * ((y + d) % NY), 128), 128)
+        f_copies.append(
+            remote(field.at[:, :, cols], fy.at[d - 1], f_s.at[d - 1], f_r.at[d - 1], y_tms[d - 1], lon)
+        )
+
+    def edge_term(side, l):
+        tiles = [lat_smooth(ohalo[side, :, c * 128:(c + 1) * 128].astype(jnp.float32)) for c in range(4)]
+        return contract_last(halves(jnp.concatenate(tiles, axis=1) * 0.0625), field[l])
+
     up.wait()
-    acc = acc + contract_last(halves(osm[1]), fhalo[0])
+    acc = acc + edge_term(0, 0)
     down.wait()
-    acc = acc + contract_last(halves(osm[bands]), fhalo[1])
+    acc = acc + edge_term(1, bands - 1)
 
     cbuf[0] = acc[:RANK] + acc[RANK:]
     copy = remote(cbuf.at[0], cbuf.at[1], core_s, core_r, tm, core_lon)
@@ -166,67 +177,78 @@
     sketch_low = (matmul(low, t_mid, HI) + matmul(raw, t_high, HI)) * has_low
     sketch_high = (matmul(raw, t_low, HI) + matmul(high, t_mid, HI)) * has_high
     back = matmul(sketch_low, t_low, HI) + matmul(sketch, t_mid, HI) + matmul(sketch_high, t_high, HI)
+    ubuf[0] = halves(back)
+    u_copies = [
+        remote(ubuf.at[0], ubuf.at[d], u_s.at[d - 1], u_r.at[d - 1], y_tms[d - 1], lon) for d in range(1, NY)
+    ]
     gram = contract_last(sketch, sketch, HI)
     gbuf[0] = jnp.concatenate([gram, jnp.zeros((RANK, 64), jnp.float32)], axis=1)
-
-    back2 = halves(back)
-
-    def term(block):
-        both = matmul(back2, block)
-        return both[:RANK] + both[RANK:]
-
-    va[0] = term(fhalo[0])
-    va[bands + 1] = term(fhalo[1])
-
-    def pattern_term(l, carry):
-        va[l + 1] = term(field[l])
+    for copy in f_copies + u_copies:
+        copy.wait()
+    back_all = jnp.concatenate([ubuf[d] for d in range(NY)], axis=1)
+    mine = pl.ds(pl.multiple_of(128 * y, 128), 128)
+
+    def pattern_terms(pair, carry):
+        blocks = []
+        for l in (2 * pair, 2 * pair + 1):
+            blocks.append(jnp.concatenate([field[l, :, mine]] + [fy[d, l] for d in range(NY - 1)], axis=0))
+        both = matmul(back_all, jnp.concatenate(blocks, axis=1))
+        both = both[:RANK] + both[RANK:]
+        for k in range(NZ):
+            rows = both[8 * k:8 * k + 8]
+            zsend[k, pair] = jnp.concatenate([rows[:, :128], rows[:, 128:]], axis=0).astype(jnp.bfloat16)
         return carry
 
-    lax.fori_loop(0, bands, pattern_term, 0)
-
-    def pack(pair, carry):
-        l = 2 * pair
-        one, two, three, four = va[l], va[l + 1], va[l + 2], va[l + 3]
-        even = one + 2.0 * two + three
-        odd = two + 2.0 * three + four
-        for c in range(NY):
-            for k in range(NZ):
-                rows, cols = slice(8 * k, 8 * k + 8), slice(128 * c, 128 * c + 128)
-                ysend[c, k, pair] = jnp.concatenate([even[rows, cols], odd[rows, cols]], axis=0).astype(jnp.bfloat16)
-        return carry
-
-    lax.fori_loop(0, bands // 2, pack, 0)
-
-    y_copies = []
-    for d in range(1, NY):
-        y_copies.append(
-            remote(ysend.at[(y + d) % NY], yrecv.at[d - 1], y_s.at[d - 1], y_r.at[d - 1], y_tms[d - 1], lon)
-        )
-
-    steps = [(1, z, 1), (2, z, 2), (4, z, 4), (1, y, NZ), (2, y, 2 * NZ)]
-    for i, (bit, coord, stride) in enumerate(steps):
-        to_tm = tm + stride - 2 * stride * ((coord // bit) % 2)
-        copy = remote(gbuf.at[i], gin.at[i], g_s.at[i], g_r.at[i], to_tm, lon)
-        copy.wait()
-        gbuf[i + 1] = gbuf[i] + gin[i]
-
-    for copy in y_copies:
-        copy.wait()
-
-    def sum_y(k, carry):
-        value = ysend[y, k].astype(jnp.float32)
-        for d in range(NY - 1):
-            value = value + yrecv[d, k].astype(jnp.float32)
-        zsend[k] = value.astype(jnp.bfloat16)
-        return carry
-
-    lax.fori_loop(0, NZ, sum_y, 0)
+    lax.fori_loop(0, bands // 2, pattern_terms, 0)
     z_copies = []
     for d in range(1, NZ):
         z_copies.append(
             remote(zsend.at[(z + d) % NZ], zrecv.at[d - 1], z_s.at[d - 1], z_r.at[d - 1], z_tms[d - 1], lon)
         )
 
+    steps = [(1, z, 1), (2, z, 2), (4, z, 4), (1, y, NZ), (2, y, 2 * NZ)]
+    for i, (bit, coord, stride) in enumerate(steps):
+        to_tm = tm + stride - 2 * stride * ((coord // bit) % 2)
+        copy = remote(gbuf.at[i], gin.at[i], g_s.at[i], g_r.at[i], to_tm, lon)
+        copy.wait()
+        gbuf[i + 1] = gbuf[i] + gin[i]
+
+    for copy in z_copies:
+        copy.wait()
+    value = zsend[z].astype(jnp.float32)
+    for d in range(NZ - 1):
+        value = value + zrecv[d].astype(jnp.float32)
+    value = lat_smooth(value.reshape(bands * 8, 128)) * 0.0625
+    lon_edge[0] = value[:8]
+    lon_edge[1] = value[bands * 8 - 8:]
+    from_high = remote(lon_edge.at[0], lon_in.at[1], le_s.at[0], le_r.at[0], tm, prev_lon)
+    from_low = remote(lon_edge.at[1], lon_in.at[0], le_s.at[1], le_r.at[1], tm, next_lon)
+    inner = value[8:-24] + 2.0 * value[16:-16] + value[24:-8]
+    gathered[y, z] = inner.reshape(bands // 2 - 2, 16, 128).astype(jnp.bfloat16)
+    y_next, y_prev = y_tms[0], y_tms[NY - 2]
+
+    def all_z(buf, send, recv):
+        return [
+            remote(buf.at[y, z], buf.at[y, z], send.at[i], recv.at[i], other, lon) for i, other in enumerate(z_tms)
+        ]
+
+    def both_y(buf, send, recv, i):
+        k = (z + NZ - i) % NZ
+        block = buf.at[y, k]
+        return [
+            remote(block, block, send.at[i, 0], recv.at[i, 0], y_next, lon),
+            remote(block, block, send.at[i, 1], recv.at[i, 1], y_prev, lon),
+        ]
+
+    def relay_y(buf, send, recv, i, pair):
+        k = (z + NZ - i) % NZ
+        way = i % 2
+        pair[way].wait_recv()
+        block = buf.at[(y + NY - 1) % NY if way == 0 else (y + 1) % NY, k]
+        copy = remote(block, block, send.at[i, 2], recv.at[i, 2], y_next if way == 0 else y_prev, lon)
+        return [pair[way].wait_send, pair[1 - way].wait, copy.wait]
+
+    az = all_z(gathered, az_s, az_r)
     lane = lax.broadcasted_iota(jnp.int32, (RANK, 128), 1)
     row_of = lax.broadcasted_iota(jnp.int32, (RANK, 128), 0)
     elim[...] = jnp.where(lane == row_of + RANK, 1.0, gbuf[len(steps)])
@@ -240,58 +262,65 @@
         elim[...] = matrix - factor * row
         return carry
 
-    lax.fori_loop(0, RANK, eliminate, 0)
+    order = (0, 1, 7, 2, 6, 3, 5, 4)
+    ends = []
+    previous = None
+    for turn, i in enumerate(order):
+        if i:
+            az[i - 1].wait_recv()
+            ends.append(az[i - 1].wait_send)
+        pair = both_y(gathered, ay_s, ay_r, i)
+        if previous is not None:
+            ends += relay_y(gathered, ay_s, ay_r, *previous)
+        previous = (i, pair)
+        if turn == 3:
+            from_low.wait()
+            from_high.wait()
+            low_rim = jnp.concatenate([lon_in[0] + 2.0 * value[:8] + value[8:16], value[:8] + 2.0 * value[8:16] + value[16:24]], axis=0)
+            high_rim = jnp.concatenate([value[-24:-16] + 2.0 * value[-16:-8] + value[-8:], value[-16:-8] + 2.0 * value[-8:] + lon_in[1]], axis=0)
+            rims[y, z] = jnp.stack([low_rim, high_rim]).astype(jnp.bfloat16)
+            rz = all_z(rims, rz_s, rz_r)
+        lax.fori_loop(8 * turn, 8 * turn + 8, eliminate, 0)
+    ends += relay_y(gathered, ay_s, ay_r, *previous)
+    pairs = []
+    for i in order:
+        if i:
+            rz[i - 1].wait_recv()
+            ends.append(rz[i - 1].wait_send)
+        pairs.append((i, both_y(rims, ry_s, ry_r, i)))
+
     matrix = elim[...]
     diagonal = jnp.sum(jnp.where(lane == row_of, matrix, 0.0), axis=1, keepdims=True)
     inverse = (matrix / jnp.sqrt(diagonal))[:, RANK:]
     basis = matmul(inverse, sketch, HI)
     series_out[...] = basis * math.sqrt(128 * days_blocks)
-    basis_out[...] = contract_first(inverse, basis, HI).astype(jnp.bfloat16)
-
-    for copy in z_copies:
-        copy.wait()
-    value = zsend[z].astype(jnp.float32)
-    for d in range(NZ - 1):
-        value = value + zrecv[d].astype(jnp.float32)
-    value = lat_smooth(value.reshape(bands // 2 * 16, 128)) * 0.0625
-    gathered[y, z] = value.reshape(bands // 2, 16, 128).astype(jnp.bfloat16)
-
-    az = [
-        remote(gathered.at[y, z], gathered.at[y, z], az_s.at[i], az_r.at[i], other, lon)
-        for i, other in enumerate(z_tms)
-    ]
-    ay = []
-
-    def over_y(i, k):
-        for d in range(1, NY):
-            ay.append(
-                remote(gathered.at[y, k], gathered.at[y, k], ay_s.at[i, d - 1], ay_r.at[i, d - 1], y_tms[d - 1], lon)
-            )
-
-    over_y(0, z)
-    for d in (1, 7, 2, 6, 3, 5, 4):
-        az[d - 1].wait_recv()
-        over_y(d, (z + NZ - d) % NZ)
-    for copy in az:
-        copy.wait_send()
-    for copy in ay:
-        copy.wait()
-
-    def unpack(pair, carry):
+    basis_out[...] = contract_first(basis, inverse, HI).astype(jnp.bfloat16)
+
+    for i, pair in pairs:
+        ends += relay_y(rims, ry_s, ry_r, i, pair)
+    for end in ends:
+        end()
+
+    def unpack_pair(source, at, pair):
         for c in range(NY):
-            both = [gathered[c, k, pair].astype(jnp.float32) for k in range(NZ)]
+            both = [source[c, k, at].astype(jnp.float32) for k in range(NZ)]
             cols = slice(128 * c, 128 * c + 128)
             for i in range(2):
                 rows = jnp.concatenate([block[8 * i:8 * i + 8] for block in both], axis=0)
                 patterns_out[2 * pair + i, :, cols] = rows.astype(jnp.bfloat16)
+
+    def unpack(pair, carry):
+        unpack_pair(gathered, pair - 1, pair)
         return carry
 
-    lax.fori_loop(0, bands // 2, unpack, 0)
+    lax.fori_loop(1, bands // 2 - 1, unpack, 0)
+    unpack_pair(rims, 0, 0)
+    unpack_pair(rims, 1, bands // 2 - 1)
 
 
 def project(basis, patterns, out):
     for i in range(patterns.shape[0]):
-        out[i] = contract_first(basis[...], patterns[i]).astype(jnp.bfloat16)
+        out[i] = matmul(basis[...], patterns[i]).astype(jnp.bfloat16)
 
 
 def local(field, omega):
@@ -299,21 +328,21 @@
     pairs = bands // 2
     f32, bf16 = jnp.float32, jnp.bfloat16
     dma = pltpu.SemaphoreType.DMA
-    chunk = (pairs, 16, 128)
     vmem = pl.BlockSpec(memory_space=pltpu.VMEM)
     patterns, basis, series = pl.pallas_call(
         kernel,
         out_shape=(
             jax.ShapeDtypeStruct((bands, RANK, cols), bf16),
-            jax.ShapeDtypeStruct((RANK, days), bf16),
+            jax.ShapeDtypeStruct((days, RANK), bf16),
             jax.ShapeDtypeStruct((RANK, days), f32),
         ),
         in_specs=[vmem] * 3,
         out_specs=(vmem,) * 3,
         scratch_shapes=[
-            pltpu.VMEM((2, days, cols), bf16),
+            pltpu.VMEM((2, RANK, cols), bf16),
             pltpu.VMEM((bands + 2, RANK, cols), f32),
-            pltpu.VMEM((bands + 2, RANK, cols), f32),
+            pltpu.VMEM((NY - 1, bands, days, 128), bf16),
+            pltpu.VMEM((NY, 2 * RANK, days), bf16),
             pltpu.VMEM((2, RANK, days), f32),
             pltpu.VMEM((NX, RANK, days), f32),
             pltpu.VMEM((2, RANK, days), f32),
@@ -321,15 +350,17 @@
             pltpu.VMEM((4, 16, days), f32),
             pltpu.VMEM((6, RANK, 128), f32),
             pltpu.VMEM((5, RANK, 128), f32),
-            pltpu.VMEM((NY, NZ) + chunk, bf16),
-            pltpu.VMEM((NY - 1, NZ) + chunk, bf16),
-            pltpu.VMEM((NZ,) + chunk, bf16),
-            pltpu.VMEM((NZ - 1,) + chunk, bf16),
-            pltpu.VMEM((NY, NZ) + chunk, bf16),
+            pltpu.VMEM((NZ, pairs, 16, 128), bf16),
+            pltpu.VMEM((NZ - 1, pairs, 16, 128), bf16),
+            pltpu.VMEM((2, 8, 128), f32),
+            pltpu.VMEM((2, 8, 128), f32),
+            pltpu.VMEM((NY, NZ, pairs - 2, 16, 128), bf16),
+            pltpu.VMEM((NY, NZ, 2, 16, 128), bf16),
             pltpu.VMEM((RANK, 128), f32),
             dma((2,)), dma((2,)), dma, dma, dma((3,)), dma((3,)), dma, dma, dma((4,)), dma((4,)),
-            dma((5,)), dma((5,)), dma((3,)), dma((3,)), dma((7,)), dma((7,)), dma((7,)), dma((7,)),
-            dma((8, 3)), dma((8, 3)),
+            dma((5,)), dma((5,)), dma((3,)), dma((3,)), dma((3,)), dma((3,)), dma((7,)), dma((7,)),
+            dma((2,)), dma((2,)), dma((7,)), dma((7,)), dma((8, 3)), dma((8, 3)),
+            dma((7,)), dma((7,)), dma((8, 3)), dma((8, 3)),
         ],
         compiler_params=pltpu.CompilerParams(collective_id=0, has_side_effects=True),
         name="subspace",
@@ -340,7 +371,7 @@
         grid=(bands // step,),
         out_shape=jax.ShapeDtypeStruct((bands, days, cols), bf16),
         in_specs=[
-            pl.BlockSpec((RANK, days), lambda i: (0, 0)),
+            pl.BlockSpec((days, RANK), lambda i: (0, 0)),
             pl.BlockSpec((step, RANK, cols), lambda i: (i, 0, 0)),
         ],
         out_specs=pl.BlockSpec((step, days, cols), lambda i: (i, 0, 0)),

time: 117 us -> 117 us (level)
  no operation moved by 1% of the time
where the time goes in v2:
time: 117 us
  Pallas kernels  116 us (99%)
    pallas_call x1, Pallas kernels, local(): pl.pallas_call(kernel, out_shape=(jax.ShapeDtypeStruct((bands, RANK, cols...  110 us
    pallas_call x1, Pallas kernels, local(): pl.pallas_call(project, grid=(bands // step,), out_shape=jax.ShapeDtypeSt...  5.2 us

profile of v2, /device:TPU:2, one launch (start us, length us, event | category | flops | bytes accessed | tf_op | source)
XLA Modules:
  0.0 116.8 jit_solution(5101548409362340898)
XLA Ops:
  0.6 110.3 %subspace.1 = (bf16[18,64,512]{2,1,0:T(8,128)(2,1)}, bf16[128,64]{1,0:T(8,128)(2,1)}, f32[64,128]{1,0:T(8,128)}) custom-call(bf16[18,128,512]{2,1,0:T(8,128)(2,1)} %bitcast.4, bf16[18,64,512]{2,1,0:T(8,128)(2,1)} %bitcast.6, f32[384,128]{1,0:T(8,128)} %constant.2.clone.toeplitz), custom_call_target="tpu_custom_call" | custom-call | tf_op jit(solution)/shard_map/subspace/pallas_call | solution.py:332
  111.0 0.0 copy-start
  111.0 5.2 %project.1 = bf16[18,128,512]{2,1,0:T(8,128)(2,1)} custom-call(bf16[128,64]{1,0:T(8,128)(2,1)} %get-tuple-element.5.basis, bf16[18,64,512]{2,1,0:T(8,128)(2,1)} %get-tuple-element.6.patterns), custom_call_target="tpu_custom_call" | custom-call | tf_op jit(solution)/shard_map/project/pallas_call | solution.py:369
  116.2 0.0 copy-done
  116.2 0.6 copy.6
Async XLA Ops:
  111.0 5.2 %copy-start = (f32[64,128]{1,0:T(8,128)S(1)}, f32[64,128]{1,0:T(8,128)}, u32[]{:S(2)}) copy-start(f32[64,128]{1,0:T(8,128)} %get-tuple-element.7) | copy-start | bytes 98308

commit v3 on v2

--- a/solution.py
+++ b/solution.py
@@ -59,8 +59,8 @@
 
 def kernel(
     field, omega, toeplitz, patterns_out, basis_out, series_out,
-    ohalo, osm, fy, ubuf, cbuf, xbuf, zq, edges, edge_in, gbuf, gin, zsend, zrecv, lon_edge, lon_in, gathered, rims, elim,
-    halo_s, halo_r, core_s, core_r, x_s, x_r, zq_s, zq_r, edge_s, edge_r, g_s, g_r, f_s, f_r, u_s, u_r, z_s, z_r,
+    ohalo, osm, fy, ubuf, cbuf, xbuf, zq, edges, edge_in, gz, gy, zsend, zrecv, lon_edge, lon_in, gathered, rims, elim,
+    halo_s, halo_r, core_s, core_r, x_s, x_r, zq_s, zq_r, edge_s, edge_r, gz_s, gz_r, gy_s, gy_r, f_s, f_r, u_s, u_r, z_s, z_r,
     le_s, le_r, az_s, az_r, ay_s, ay_r, rz_s, rz_r, ry_s, ry_r,
 ):
     bands = field.shape[0]
@@ -177,12 +177,15 @@
     sketch_low = (matmul(low, t_mid, HI) + matmul(raw, t_high, HI)) * has_low
     sketch_high = (matmul(raw, t_low, HI) + matmul(high, t_mid, HI)) * has_high
     back = matmul(sketch_low, t_low, HI) + matmul(sketch, t_mid, HI) + matmul(sketch_high, t_high, HI)
+    gram = contract_last(sketch, sketch, HI)
+    gz[z] = jnp.concatenate([gram[:32], gram[32:]], axis=1)
+    gz_copies = [
+        remote(gz.at[z], gz.at[z], gz_s.at[i], gz_r.at[i], other, lon) for i, other in enumerate(z_tms)
+    ]
     ubuf[0] = halves(back)
     u_copies = [
         remote(ubuf.at[0], ubuf.at[d], u_s.at[d - 1], u_r.at[d - 1], y_tms[d - 1], lon) for d in range(1, NY)
     ]
-    gram = contract_last(sketch, sketch, HI)
-    gbuf[0] = jnp.concatenate([gram, jnp.zeros((RANK, 64), jnp.float32)], axis=1)
     for copy in f_copies + u_copies:
         copy.wait()
     back_all = jnp.concatenate([ubuf[d] for d in range(NY)], axis=1)
@@ -206,12 +209,33 @@
             remote(zsend.at[(z + d) % NZ], zrecv.at[d - 1], z_s.at[d - 1], z_r.at[d - 1], z_tms[d - 1], lon)
         )
 
-    steps = [(1, z, 1), (2, z, 2), (4, z, 4), (1, y, NZ), (2, y, 2 * NZ)]
-    for i, (bit, coord, stride) in enumerate(steps):
-        to_tm = tm + stride - 2 * stride * ((coord // bit) % 2)
-        copy = remote(gbuf.at[i], gin.at[i], g_s.at[i], g_r.at[i], to_tm, lon)
-        copy.wait()
-        gbuf[i + 1] = gbuf[i] + gin[i]
+    for copy in gz_copies:
+        copy.wait()
+    part = gz[0]
+    for k in range(1, NZ):
+        part = part + gz[k]
+    gy[y] = part
+    gy_copies = [
+        remote(gy.at[y], gy.at[y], gy_s.at[i], gy_r.at[i], other, lon) for i, other in enumerate(y_tms)
+    ]
+    for copy in gy_copies:
+        copy.wait()
+    part = (gy[0] + gy[1]) + (gy[2] + gy[3])
+    lane = lax.broadcasted_iota(jnp.int32, (RANK, 128), 1)
+    row_of = lax.broadcasted_iota(jnp.int32, (RANK, 128), 0)
+    stacked = jnp.concatenate([part, pltpu.roll(part, 64, 1)], axis=0)
+    elim[...] = jnp.where(lane < RANK, stacked, jnp.where(lane == row_of + RANK, 1.0, 0.0))
+
+    def eliminate(j, carry):
+        matrix = elim[...]
+        row = elim[pl.ds(j, 1), :]
+        column = jnp.sum(jnp.where(lane == j, matrix, 0.0), axis=1, keepdims=True)
+        pivot = jnp.sum(jnp.where(lane[:1] == j, row, 0.0), axis=1, keepdims=True)
+        factor = jnp.where(row_of[:, :1] > j, column / pivot, 0.0)
+        elim[...] = matrix - factor * row
+        return carry
+
+    lax.fori_loop(0, RANK, eliminate, 0)
 
     for copy in z_copies:
         copy.wait()
@@ -249,19 +273,6 @@
         return [pair[way].wait_send, pair[1 - way].wait, copy.wait]
 
     az = all_z(gathered, az_s, az_r)
-    lane = lax.broadcasted_iota(jnp.int32, (RANK, 128), 1)
-    row_of = lax.broadcasted_iota(jnp.int32, (RANK, 128), 0)
-    elim[...] = jnp.where(lane == row_of + RANK, 1.0, gbuf[len(steps)])
-
-    def eliminate(j, carry):
-        matrix = elim[...]
-        row = elim[pl.ds(j, 1), :]
-        column = jnp.sum(jnp.where(lane == j, matrix, 0.0), axis=1, keepdims=True)
-        pivot = jnp.sum(jnp.where(lane[:1] == j, row, 0.0), axis=1, keepdims=True)
-        factor = jnp.where(row_of[:, :1] > j, column / pivot, 0.0)
-        elim[...] = matrix - factor * row
-        return carry
-
     order = (0, 1, 7, 2, 6, 3, 5, 4)
     ends = []
     previous = None
@@ -273,14 +284,13 @@
         if previous is not None:
             ends += relay_y(gathered, ay_s, ay_r, *previous)
         previous = (i, pair)
-        if turn == 3:
+        if turn == 5:
             from_low.wait()
             from_high.wait()
             low_rim = jnp.concatenate([lon_in[0] + 2.0 * value[:8] + value[8:16], value[:8] + 2.0 * value[8:16] + value[16:24]], axis=0)
             high_rim = jnp.concatenate([value[-24:-16] + 2.0 * value[-16:-8] + value[-8:], value[-16:-8] + 2.0 * value[-8:] + lon_in[1]], axis=0)
             rims[y, z] = jnp.stack([low_rim, high_rim]).astype(jnp.bfloat16)
             rz = all_z(rims, rz_s, rz_r)
-        lax.fori_loop(8 * turn, 8 * turn + 8, eliminate, 0)
     ends += relay_y(gathered, ay_s, ay_r, *previous)
     pairs = []
     for i in order:
@@ -348,8 +358,8 @@
             pltpu.VMEM((2, RANK, days), f32),
             pltpu.VMEM((2, 16, days), f32),
             pltpu.VMEM((4, 16, days), f32),
-            pltpu.VMEM((6, RANK, 128), f32),
-            pltpu.VMEM((5, RANK, 128), f32),
+            pltpu.VMEM((NZ, 32, 128), f32),
+            pltpu.VMEM((NY, 32, 128), f32),
             pltpu.VMEM((NZ, pairs, 16, 128), bf16),
             pltpu.VMEM((NZ - 1, pairs, 16, 128), bf16),
             pltpu.VMEM((2, 8, 128), f32),
@@ -358,7 +368,7 @@
             pltpu.VMEM((NY, NZ, 2, 16, 128), bf16),
             pltpu.VMEM((RANK, 128), f32),
             dma((2,)), dma((2,)), dma, dma, dma((3,)), dma((3,)), dma, dma, dma((4,)), dma((4,)),
-            dma((5,)), dma((5,)), dma((3,)), dma((3,)), dma((3,)), dma((3,)), dma((7,)), dma((7,)),
+            dma((7,)), dma((7,)), dma((3,)), dma((3,)), dma((3,)), dma((3,)), dma((3,)), dma((3,)), dma((7,)), dma((7,)),
             dma((2,)), dma((2,)), dma((7,)), dma((7,)), dma((8, 3)), dma((8, 3)),
             dma((7,)), dma((7,)), dma((8, 3)), dma((8, 3)),
         ],

time: 117 us -> 111 us (0.949)
  Pallas kernels: 116 us -> 109 us
    pallas_call x1, Pallas kernels: 110 us -> 104 us  [local(): pl.pallas_call(kernel, out_shape=(jax.ShapeDtypeStruct((bands, RANK, cols...]
where the time goes in v3:
time: 111 us; the launch traced here: 110 us
  Pallas kernels  109 us (98%)
    pallas_call x1, Pallas kernels, local(): pl.pallas_call(kernel, out_shape=(jax.ShapeDtypeStruct((bands, RANK, cols...  104 us
    pallas_call x1, Pallas kernels, local(): pl.pallas_call(project, grid=(bands // step,), out_shape=jax.ShapeDtypeSt...  5.19 us

profile of v3, /device:TPU:2, one launch (start us, length us, event | category | flops | bytes accessed | tf_op | source)
XLA Modules:
  0.0 110.5 jit_solution(8807490261324130286)
XLA Ops:
  0.6 104.0 %subspace.1 = (bf16[18,64,512]{2,1,0:T(8,128)(2,1)}, bf16[128,64]{1,0:T(8,128)(2,1)}, f32[64,128]{1,0:T(8,128)}) custom-call(bf16[18,128,512]{2,1,0:T(8,128)(2,1)} %bitcast.4, bf16[18,64,512]{2,1,0:T(8,128)(2,1)} %bitcast.6, f32[384,128]{1,0:T(8,128)} %constant.2.clone.toeplitz), custom_call_target="tpu_custom_call" | custom-call | tf_op jit(solution)/shard_map/subspace/pallas_call | solution.py:342
  104.6 0.0 copy-start
  104.7 5.2 %project.1 = bf16[18,128,512]{2,1,0:T(8,128)(2,1)} custom-call(bf16[128,64]{1,0:T(8,128)(2,1)} %get-tuple-element.5.basis, bf16[18,64,512]{2,1,0:T(8,128)(2,1)} %get-tuple-element.6.patterns), custom_call_target="tpu_custom_call" | custom-call | tf_op jit(solution)/shard_map/project/pallas_call | solution.py:379
  109.8 0.0 copy-done
  109.9 0.6 copy.6
Async XLA Ops:
  104.6 5.2 %copy-start = (f32[64,128]{1,0:T(8,128)S(1)}, f32[64,128]{1,0:T(8,128)}, u32[]{:S(2)}) copy-start(f32[64,128]{1,0:T(8,128)} %get-tuple-element.7) | copy-start | bytes 98308

commit v4 on v3

--- a/solution.py
+++ b/solution.py
@@ -375,7 +375,7 @@
         compiler_params=pltpu.CompilerParams(collective_id=0, has_side_effects=True),
         name="subspace",
     )(jnp.transpose(field, (1, 0, 2)), jnp.transpose(omega, (0, 2, 1)), jnp.asarray(toeplitz_blocks()))
-    step = 3
+    step = 6
     projected = pl.pallas_call(
         project,
         grid=(bands // step,),

time: 111 us -> 109 us (0.982)
    pallas_call x1, Pallas kernels: 5.19 us -> 3.87 us  [local(): pl.pallas_call(project, grid=(bands // step,), out_shape=jax.ShapeDtypeSt...]
where the time goes in v4:
time: 109 us
  Pallas kernels  108 us (99%)
    pallas_call x1, Pallas kernels, local(): pl.pallas_call(kernel, out_shape=(jax.ShapeDtypeStruct((bands, RANK, cols...  104 us
    pallas_call x1, Pallas kernels, local(): pl.pallas_call(project, grid=(bands // step,), out_shape=jax.ShapeDtypeSt...  3.87 us

profile of v4, /device:TPU:2, one launch (start us, length us, event | category | flops | bytes accessed | tf_op | source)
XLA Modules:
  0.0 109.1 jit_solution(14006962609970672145)
XLA Ops:
  0.6 104.0 %subspace.1 = (bf16[18,64,512]{2,1,0:T(8,128)(2,1)}, bf16[128,64]{1,0:T(8,128)(2,1)}, f32[64,128]{1,0:T(8,128)}) custom-call(bf16[18,128,512]{2,1,0:T(8,128)(2,1)} %bitcast.4, bf16[18,64,512]{2,1,0:T(8,128)(2,1)} %bitcast.6, f32[384,128]{1,0:T(8,128)} %constant.2.clone.toeplitz), custom_call_target="tpu_custom_call" | custom-call | tf_op jit(solution)/shard_map/subspace/pallas_call | solution.py:342
  104.6 0.0 copy-start
  104.7 3.9 %project.1 = bf16[18,128,512]{2,1,0:T(8,128)(2,1)} custom-call(bf16[128,64]{1,0:T(8,128)(2,1)} %get-tuple-element.5.basis, bf16[18,64,512]{2,1,0:T(8,128)(2,1)} %get-tuple-element.6.patterns), custom_call_target="tpu_custom_call" | custom-call | tf_op jit(solution)/shard_map/project/pallas_call | solution.py:379
  108.5 0.0 copy-done
  108.5 0.6 copy.6
Async XLA Ops:
  104.6 3.9 %copy-start = (f32[64,128]{1,0:T(8,128)S(1)}, f32[64,128]{1,0:T(8,128)}, u32[]{:S(2)}) copy-start(f32[64,128]{1,0:T(8,128)} %get-tuple-element.7) | copy-start | bytes 98308
